TPU v7x, 32 devices: a whole 2x2x4 slice. The times are simulated.
32 devices in a mesh: survey: 2 (over x), depth: 16 (over z, y, core).
Axes of the slice: x: 2, y: 2, z: 4, core: 2. Of those that a mesh axis runs over, the one named last changes fastest.
Arguments:
- arriving: float32 [32, 2, 2, 4, 128, 128], P(('survey', 'depth')), parts along dimension 0, may hold values from -3.1 to 3.1
- classes: int32 [16, 128, 128], P('depth'), may hold values from 0 to 15
- filters: float32 [18, 4, 2, 6, 16], replicated, may hold values from -1.25 to 1.25
- src_pos: int32 [4, 4, 2], P('survey'), parts along dimension 0, may hold values from 0 to 127
- wavelet: float32 [4, 4, 2, 4], P('survey'), parts along dimension 0, may hold values from -6 to 6
- rec_pos: int32 [1024, 2], P('survey'), parts along dimension 0, may hold values from 0 to 127
- rec_data: float32 [4, 2, 4, 512], P('survey'), parts along dimension 0, may hold values from -6 to 6
Outputs:
- image: float32 [32, 128, 128], P(('survey', 'depth')), parts along dimension 0
- passing: float32 [32, 2, 2, 4, 128, 128], P(('survey', 'depth')), parts along dimension 0
There are 2 independent parts, one for each index of `survey`. A program takes and returns all parts, laid end to end along the dimension named above; an argument that names none is the same for every part. Nothing has to cross between parts.
All inputs are finite; a program needn't handle non-finite values.
Results may differ from a plain program's by a relative error of at most 0.0001.
Values sent between devices are 32-bit elements; how exact they have to be, the bound alone decides.
A program may use at most 64 MiB of HBM per device.

v0:
```python
import functools
import math

import jax
import jax.numpy as jnp
from jax import lax
from jax.experimental import pallas as pl
from jax.experimental.pallas import tpu as pltpu
from jax.sharding import PartitionSpec as P

MESH = pl.DeviceIdType.MESH
PAD = 8


def kernel(
    chain,
    ticks,
    freqs,
    terms,
    width,
    src_pos,
    wavelet,
    arriving,
    classes,
    filters,
    rec_pos,
    rec_data,
    image,
    passing,
    fields,
    leaving,
    table,
    coef,
    terms_buf,
    corr,
    illum,
    totals,
    rec_x,
    rec_y,
    in_sem,
    table_sem,
    out_sem,
    send_sem,
    recv_sem,
    tot_send,
    tot_recv,
):
    position = lax.axis_index("depth")
    has_next = position < chain - 1
    following_slab = lax.rem(position + 1, chain)
    is_first = position == 0

    def load_copy(kind, freq):
        return pltpu.make_async_copy(
            arriving.at[0, kind, :, freq], fields.at[0, kind, :, freq], in_sem.at[kind, freq]
        )

    def send_copy(tick, kind, freq):
        return pltpu.make_async_remote_copy(
            src_ref=leaving.at[tick, kind, :, freq],
            dst_ref=fields.at[tick + 1, kind, :, freq],
            send_sem=send_sem.at[tick, kind, freq],
            recv_sem=recv_sem.at[tick, kind, freq],
            device_id={"depth": following_slab},
            device_id_type=MESH,
        )

    def out_copy(kind, freq):
        return pltpu.make_async_copy(
            leaving.at[ticks - 1, kind, :, freq],
            passing.at[0, kind, :, freq],
            out_sem.at[kind, freq],
        )

    def total_copy(other):
        return pltpu.make_async_remote_copy(
            src_ref=totals.at[position],
            dst_ref=totals.at[position],
            send_sem=tot_send.at[other],
            recv_sem=tot_recv.at[position],
            device_id={"depth": other},
            device_id_type=MESH,
        )

    def total_arrival(other):
        return pltpu.make_async_remote_copy(
            src_ref=totals.at[other],
            dst_ref=totals.at[other],
            send_sem=tot_send.at[other],
            recv_sem=tot_recv.at[other],
            device_id={"depth": other},
            device_id_type=MESH,
        )

    table_copy = pltpu.make_async_copy(
        filters.at[pl.ds(chain - 1 - position, ticks)], table, table_sem
    )
    table_copy.start()
    for kind in range(2):
        for freq in range(freqs):
            load_copy(kind, freq).start()

    barrier = pltpu.get_barrier_semaphore()

    @pl.loop(1, chain)
    def _(step):
        pl.semaphore_signal(
            barrier,
            inc=1,
            device_id={"depth": lax.rem(position + step, chain)},
            device_id_type=MESH,
        )

    corr[...] = jnp.zeros_like(corr)
    illum[...] = jnp.zeros_like(illum)
    edge = jnp.zeros((2, terms, PAD, width), jnp.float32)
    terms_buf[:, :, 0:PAD, :] = edge
    terms_buf[:, :, PAD + width : 2 * PAD + width, :] = edge
    table_copy.wait()

    def gather_coefficients(tick, freq):
        cells = classes[0]
        for part in range(2):
            rows = table[tick, freq, part]
            rows = jnp.concatenate(
                [rows, jnp.zeros((terms, width - rows.shape[1]), jnp.float32)], axis=1
            )
            for term in range(terms):
                row = jnp.broadcast_to(rows[term : term + 1, :], (width, width))
                coef[freq, part, term] = jnp.take_along_axis(
                    row, cells, axis=1, mode="promise_in_bounds"
                )

    lane = lax.broadcasted_iota(jnp.int32, (width, width), 1)
    first_lane = lane == 0
    last_lane = lane == width - 1

    def smooth(part, term):
        centre = terms_buf[part, term, PAD : PAD + width, :]
        rows = (
            terms_buf[part, term, PAD - 1 : PAD - 1 + width, :]
            + terms_buf[part, term, PAD + 1 : PAD + 1 + width, :]
        ) + (centre + centre)
        left = jnp.where(first_lane, 0.0, pltpu.roll(rows, 1, 1))
        right = jnp.where(last_lane, 0.0, pltpu.roll(rows, width - 1, 1))
        return centre, (left + right) + (rows + rows)

    def depth_step(tick, kind, freq):
        sign = 1.0 if kind == 0 else -1.0
        for part in range(2):
            terms_buf[part, 0, PAD : PAD + width, :] = fields[tick, kind, part, freq]
        for term in range(1, terms):
            for part in range(2):
                centre, total = smooth(part, term - 1)
                if term == 1:
                    value = 0.125 * total - centre
                else:
                    previous = terms_buf[part, term - 2, PAD : PAD + width, :]
                    value = 0.25 * total - ((centre + centre) + previous)
                terms_buf[part, term, PAD : PAD + width, :] = value
        for tile in range(0, width, 16):
            cells = slice(tile, tile + 16)
            padded = slice(PAD + tile, PAD + tile + 16)
            real, imag = 0.0, 0.0
            for term in range(terms):
                c_real = coef[freq, 0, term, cells, :]
                c_imag = sign * coef[freq, 1, term, cells, :]
                q_real = terms_buf[0, term, padded, :]
                q_imag = terms_buf[1, term, padded, :]
                real = real + (c_real * q_real - c_imag * q_imag)
                imag = imag + (c_real * q_imag + c_imag * q_real)
            leaving[tick, kind, 0, freq, cells, :] = real
            leaving[tick, kind, 1, freq, cells, :] = imag

    def inject(tick):
        column = lax.broadcasted_iota(jnp.int32, rec_y.shape, 1)
        if tick == 0:
            hits_x = (rec_pos[:, 0:1] == column).astype(jnp.float32)
            rec_x[...] = jnp.transpose(hits_x)
            rec_y[...] = (rec_pos[:, 1:2] == column).astype(jnp.float32)
        grid_x = lax.broadcasted_iota(jnp.int32, (width, width), 0)
        grid_y = lax.broadcasted_iota(jnp.int32, (width, width), 1)
        hits = [
            (grid_x == src_pos[tick, e, 0]) & (grid_y == src_pos[tick, e, 1])
            for e in range(src_pos.shape[1])
        ]
        for part in range(2):
            for freq in range(freqs):
                plane = jnp.zeros((width, width), jnp.float32)
                for e, hit in enumerate(hits):
                    plane = plane + jnp.where(hit, wavelet[tick, e, part, freq], 0.0)
                fields[tick + 1, 0, part, freq] = plane
                weights = rec_data[tick, part, freq : freq + 1, :]
                fields[tick + 1, 1, part, freq] = jnp.dot(
                    rec_x[...] * weights,
                    rec_y[...],
                    precision=lax.Precision.HIGHEST,
                    preferred_element_type=jnp.float32,
                )

    for tick in range(ticks):
        if tick > 0:
            pl.when(is_first)(functools.partial(inject, tick - 1))
        for kind in range(2):

            def chunk(freq, carry, tick=tick, kind=kind):
                if kind == 0:
                    gather_coefficients(tick, freq)
                if tick == 0:
                    load_copy(kind, freq).wait()
                else:

                    @pl.when(position > 0)
                    def _():
                        send_copy(tick - 1, kind, freq).wait_recv()

                depth_step(tick, kind, freq)
                if tick == 0 and kind == 0:

                    @pl.when(freq == 0)
                    def _():
                        pl.semaphore_wait(barrier, chain - 1)

                if tick < ticks - 1:

                    @pl.when(has_next)
                    def _():
                        send_copy(tick, kind, freq).start()
                else:
                    out_copy(kind, freq).start()
                real = fields[tick, 0, 0, freq]
                imag = fields[tick, 0, 1, freq]
                if kind == 0:
                    illum[...] += real * real + imag * imag
                else:
                    corr[...] += real * fields[tick, 1, 0, freq] + imag * fields[tick, 1, 1, freq]
                return carry

            lax.fori_loop(0, freqs, chunk, 0)
            if tick == ticks - 1 and kind == 0:
                totals[position] = jnp.sum(illum[...].reshape(width // 8, 8, width), axis=0)

                @pl.loop(1, chain)
                def _(step):
                    total_copy(lax.rem(position + step, chain)).start()

    @pl.loop(1, chain)
    def _(step):
        total_arrival(lax.rem(position + step, chain)).wait_recv()

    energy = jnp.sum(jnp.sum(totals[...], axis=0), keepdims=True)
    damping = energy / (chain * width * width)
    image[0] = math.sqrt(ticks * freqs) * corr[...] / (illum[...] + damping)

    @pl.loop(1, chain)
    def _(step):
        total_copy(lax.rem(position + step, chain)).wait_send()

    for kind in range(2):
        for freq in range(freqs):
            for tick in range(ticks - 1):

                @pl.when(has_next)
                def _():
                    send_copy(tick, kind, freq).wait_send()

            out_copy(kind, freq).wait()


def solution(mesh):
    chain = mesh.shape["depth"]

    def body(arriving, classes, filters, src_pos, wavelet, rec_pos, rec_data):
        _, kinds, parts, freqs, width, _ = arriving.shape
        ticks = wavelet.shape[0] + 1
        terms, labels = filters.shape[3:]
        receivers = rec_pos.shape[0]
        f32 = jnp.float32
        vmem = pl.BlockSpec(memory_space=pltpu.VMEM)
        smem = pl.BlockSpec(memory_space=pltpu.SMEM)
        hbm = pl.BlockSpec(memory_space=pl.ANY)
        window = (ticks, kinds, parts, freqs, width, width)
        return pl.pallas_call(
            functools.partial(kernel, chain, ticks, freqs, terms, width),
            out_shape=(
                jax.ShapeDtypeStruct((1, width, width), f32),
                jax.ShapeDtypeStruct(arriving.shape, f32),
            ),
            in_specs=[smem, smem, hbm, vmem, hbm, vmem, vmem],
            out_specs=(vmem, hbm),
            scratch_shapes=[
                pltpu.VMEM(window, f32),
                pltpu.VMEM(window, f32),
                pltpu.VMEM((ticks, freqs, parts, terms, labels), f32),
                pltpu.VMEM((freqs, parts, terms, width, width), f32),
                pltpu.VMEM((parts, terms, width + 2 * PAD, width), f32),
                pltpu.VMEM((width, width), f32),
                pltpu.VMEM((width, width), f32),
                pltpu.VMEM((chain, 8, width), f32),
                pltpu.VMEM((width, receivers), f32),
                pltpu.VMEM((receivers, width), f32),
                pltpu.SemaphoreType.DMA((kinds, freqs)),
                pltpu.SemaphoreType.DMA,
                pltpu.SemaphoreType.DMA((kinds, freqs)),
                pltpu.SemaphoreType.DMA((ticks - 1, kinds, freqs)),
                pltpu.SemaphoreType.DMA((ticks - 1, kinds, freqs)),
                pltpu.SemaphoreType.DMA((chain,)),
                pltpu.SemaphoreType.DMA((chain,)),
            ],
            compiler_params=pltpu.CompilerParams(
                collective_id=0, has_side_effects=True, vmem_limit_bytes=40 << 20
            ),
        )(src_pos, wavelet, arriving, classes, filters, rec_pos, rec_data)

    return jax.shard_map(
        body,
        mesh=mesh,
        in_specs=(
            P(("survey", "depth"), None, None, None, None, None),
            P("depth", None, None),
            P(),
            P("survey", None, None),
            P("survey", None, None, None),
            P("survey", None),
            P("survey", None, None, None),
        ),
        out_specs=(
            P(("survey", "depth"), None, None),
            P(("survey", "depth"), None, None, None, None, None),
        ),
        check_vma=False,
    )
```

profile of v0, /device:TPU:0, one launch (start us, length us, event | category | flops | bytes accessed | tf_op | source)
XLA Modules:
  0.0 40.8 jit_solution(14009411961243862447)
XLA Ops:
  0.6 0.0 copy-start.4
  0.6 0.0 copy-start
  0.6 0.9 %copy.9.src_pos = s32[2,4,2]{2,1,0:T(4,128)S(1)} copy(s32[2,4,2]{1,2,0:T(2,128)} %param.10) | data formatting | bytes 128 | tf_op args[3]
  1.5 0.0 copy-done.4
  1.5 0.1 copy.11.rec_pos
  1.7 0.0 copy-start.1
  1.7 0.0 copy-start.2
  1.7 0.0 copy-start.3
  1.7 1.7 %copy.10.filters = f32[18,4,2,6,16]{4,3,2,1,0:T(8,128)S(1)} copy(f32[18,4,2,6,16]{0,4,3,2,1:T(8,128)} %param.9) | data formatting | bytes 110592 | tf_op args[2]
  3.4 0.0 copy-done
  3.4 0.0 copy-done.1
  3.4 0.0 copy-done.2
  3.4 0.0 copy-done.3
  3.4 35.8 %shard_map.86 = (f32[1,128,128]{2,1,0:T(8,128)S(1)}, f32[1,2,2,4,128,128]{5,4,3,2,1,0:T(8,128)S(1)}) custom-call(s32[2,4,2]{2,1,0:T(4,128)S(1)} %copy.9.src_pos, f32[2,4,2,4]{3,2,1,0:T(2,128)S(1)} %copy-done.3, f32[1,2,2,4,128,128]{5,4,3,2,1,0:T(8,128)S(1)} %copy-done, s32[1,128,128]{2,1,0:T(8,128)S(1)} %copy-done.1, f32[18,4,2,6,16]{4,3,2,1,0:T(8,128)S(1)} %copy.10.filters, ...), custom_call_target="tpu_custom_call" | custom-call | tf_op jit(solution)/shard_map/pallas_call | solution.py:283
  39.2 0.6 %copy.14 = f32[1,128,128]{2,1,0:T(8,128)} copy(f32[1,128,128]{2,1,0:T(8,128)S(1)} %get-tuple-element.4) | data formatting | bytes 131072
  39.8 1.0 %copy.15 = f32[1,2,2,4,128,128]{5,4,3,2,1,0:T(8,128)} copy(f32[1,2,2,4,128,128]{5,4,3,2,1,0:T(8,128)S(1)} %get-tuple-element.5) | data formatting | bytes 2097152
Async XLA Ops:
  0.6 0.9 %copy-start.4 = (s32[512,2]{0,1:T(2,128)S(1)}, s32[512,2]{0,1:T(2,128)}, u32[]{:S(2)}) copy-start(s32[512,2]{0,1:T(2,128)} %param.12) | copy-start | bytes 12292
  0.6 2.7 %copy-start = (f32[1,2,2,4,128,128]{5,4,3,2,1,0:T(8,128)S(1)}, f32[1,2,2,4,128,128]{5,4,3,2,1,0:T(8,128)}, u32[]{:S(2)}) copy-start(f32[1,2,2,4,128,128]{5,4,3,2,1,0:T(8,128)} %arriving.1) | copy-start | bytes 3145732
  1.7 1.7 %copy-start.1 = (s32[1,128,128]{2,1,0:T(8,128)S(1)}, s32[1,128,128]{2,1,0:T(8,128)}, u32[]{:S(2)}) copy-start(s32[1,128,128]{2,1,0:T(8,128)} %classes.1) | copy-start | bytes 196612
  1.7 1.7 %copy-start.2 = (f32[2,2,4,512]{3,2,1,0:T(4,128)S(1)}, f32[2,2,4,512]{3,2,1,0:T(4,128)}, u32[]{:S(2)}) copy-start(f32[2,2,4,512]{3,2,1,0:T(4,128)} %rec_data.1) | copy-start | bytes 98308
  1.7 1.7 %copy-start.3 = (f32[2,4,2,4]{3,2,1,0:T(2,128)S(1)}, f32[2,4,2,4]{3,2,1,0:T(2,128)}, u32[]{:S(2)}) copy-start(f32[2,4,2,4]{3,2,1,0:T(2,128)} %wavelet.1) | copy-start | bytes 772
where the time goes:
time: 41 us; the launch traced here: 40.8 us
  Pallas kernels  35.8 us (87%)
  local copies, waits for them, and re-layouts  4.32 us (11%)
  between operations  0.71 us (2%)
    pallas_call x1, Pallas kernels, body(): pl.pallas_call(functools.partial(kernel, chain, ticks, freqs, terms, widt...  35.8 us
    unnamed x15, local copies, waits for them, and re-layouts  4.32 us

commit v1 on v0

v1 whole, which is shorter than its diff:
```python
import functools
import math

import jax
import jax.numpy as jnp
from jax import lax
from jax.experimental import pallas as pl
from jax.experimental.pallas import tpu as pltpu
from jax.sharding import PartitionSpec as P

MESH = pl.DeviceIdType.MESH
PAD = 8
ROWS = 16


def kernel(
    chain,
    ticks,
    freqs,
    terms,
    labels,
    width,
    src_pos_in,
    wavelet_in,
    arriving,
    classes_in,
    filters_in,
    rec_pos_in,
    rec_data_in,
    image,
    passing,
    src_pos,
    wavelet,
    classes,
    filters,
    rec_pos,
    rec_data,
    fields,
    leaving,
    table,
    coef,
    terms_buf,
    corr,
    illum,
    running,
    landed,
    in_sem,
    small_sem,
    out_sem,
    send_sem,
    recv_sem,
    tot_send,
    tot_recv,
):
    position = lax.axis_index("depth")
    has_next = position < chain - 1
    following_slab = lax.rem(position + 1, chain)
    is_first = position == 0

    def load_copy(kind, freq):
        return pltpu.make_async_copy(
            arriving.at[0, kind, :, freq], fields.at[0, kind, :, freq], in_sem.at[kind, freq]
        )

    def send_copy(tick, kind, freq):
        return pltpu.make_async_remote_copy(
            src_ref=leaving.at[tick, kind, :, freq],
            dst_ref=fields.at[tick + 1, kind, :, freq],
            send_sem=send_sem.at[tick, kind, freq],
            recv_sem=recv_sem.at[tick, kind, freq],
            device_id={"depth": following_slab},
            device_id_type=MESH,
        )

    def out_copy(kind, freq):
        return pltpu.make_async_copy(
            leaving.at[ticks - 1, kind, :, freq],
            passing.at[0, kind, :, freq],
            out_sem.at[kind, freq],
        )

    stages = chain.bit_length() - 1

    def partner(stage):
        distance = 1 << stage
        upper = lax.rem(position // distance, 2)
        return position + distance - 2 * distance * upper

    def total_copy(stage):
        return pltpu.make_async_remote_copy(
            src_ref=running.at[stage],
            dst_ref=landed.at[stage],
            send_sem=tot_send.at[stage],
            recv_sem=tot_recv.at[stage],
            device_id={"depth": partner(stage)},
            device_id_type=MESH,
        )

    def exchange(stage):
        if stage > 0:
            total_copy(stage - 1).wait_recv()
            running[stage] = running[stage - 1] + landed[stage - 1]
        if stage < stages:
            total_copy(stage).start()

    pairs = (
        (filters_in, filters),
        (classes_in, classes),
        (src_pos_in, src_pos),
        (wavelet_in, wavelet),
        (rec_pos_in, rec_pos),
        (rec_data_in, rec_data),
    )
    small = [
        pltpu.make_async_copy(here, there, small_sem.at[i]) for i, (here, there) in enumerate(pairs)
    ]
    small[0].start()
    small[1].start()
    for kind in range(2):
        for freq in range(freqs):
            load_copy(kind, freq).start()

    barrier = pltpu.get_barrier_semaphore()

    greeted = [(partner(stage), None) for stage in range(stages)]
    odd = lax.rem(position, 2)
    greeted.append((position + 1, (odd == 1) & (position < chain - 1)))
    greeted.append((position - 1, (odd == 0) & (position > 0)))
    for other, condition in greeted:

        def greet(other=other):
            pl.semaphore_signal(barrier, inc=1, device_id={"depth": other}, device_id_type=MESH)

        if condition is None:
            greet()
        else:
            pl.when(condition)(greet)
    end = (position == 0) | (position == chain - 1)
    greetings = stages + 1 - end.astype(jnp.int32)
    for copy in small[2:]:
        copy.start()

    corr[...] = jnp.zeros_like(corr)
    illum[...] = jnp.zeros_like(illum)
    edge = jnp.zeros((2, terms, PAD, width), jnp.float32)
    terms_buf[:, :, 0:PAD, :] = edge
    terms_buf[:, :, PAD + width : 2 * PAD + width, :] = edge
    small[0].wait()
    groups = width // labels
    for group in range(filters.shape[0] // width):
        rows = filters[group * width : (group + 1) * width, :]
        rows = jnp.concatenate(
            [rows, jnp.zeros((width, width - rows.shape[1]), jnp.float32)], axis=1
        )
        blocks = jnp.transpose(rows)[: table.shape[1], :]
        for slot in range(groups):
            shifted = blocks if slot == 0 else pltpu.roll(blocks, width - slot * labels, 1)
            table[group * groups + slot] = shifted

    def gather_coefficients(tick, freq):
        block = tick - position + chain - 1
        rows = [
            jnp.broadcast_to(table[freq * (2 * terms) + item, pl.ds(block, 1), :], (8, width))
            for item in range(2 * terms)
        ]
        for tile in range(0, width, 8):
            cells = classes[0, tile : tile + 8, :]
            for item in range(2 * terms):
                coef[tick, freq, item // terms, item % terms, tile : tile + 8, :] = jnp.take_along_axis(
                    rows[item], cells, axis=1, mode="promise_in_bounds"
                )

    lane = lax.broadcasted_iota(jnp.int32, (ROWS, width), 1)
    first_lane = lane == 0
    last_lane = lane == width - 1

    def depth_step(tick, kind, freq):
        target = leaving.at[tick]
        tiles = range(0, width, ROWS)
        for part in range(2):
            for tile in tiles:
                terms_buf[part, 0, PAD + tile : PAD + tile + ROWS, :] = fields[
                    tick, kind, part, freq, tile : tile + ROWS, :
                ]
        for term in range(1, terms):
            for part in range(2):
                for tile in tiles:
                    low = PAD + tile
                    centre = terms_buf[part, term - 1, low : low + ROWS, :]
                    twice = centre + centre
                    rows = (
                        terms_buf[part, term - 1, low - 1 : low - 1 + ROWS, :]
                        + terms_buf[part, term - 1, low + 1 : low + 1 + ROWS, :]
                    ) + twice
                    left = jnp.where(first_lane, 0.0, pltpu.roll(rows, 1, 1))
                    right = jnp.where(last_lane, 0.0, pltpu.roll(rows, width - 1, 1))
                    total = (left + right) + (rows + rows)
                    if term == 1:
                        value = 0.125 * total - centre
                    else:
                        previous = terms_buf[part, term - 2, low : low + ROWS, :]
                        value = 0.25 * total - (twice + previous)
                    terms_buf[part, term, low : low + ROWS, :] = value
        for tile in tiles:
            cells = slice(tile, tile + ROWS)
            padded = slice(PAD + tile, PAD + tile + ROWS)
            real, imag = None, None
            for term in range(terms):
                c_real = coef[tick, freq, 0, term, cells, :]
                c_imag = coef[tick, freq, 1, term, cells, :]
                q_real = terms_buf[0, term, padded, :]
                q_imag = terms_buf[1, term, padded, :]
                if kind == 0:
                    new_real = c_real * q_real - c_imag * q_imag
                    new_imag = c_real * q_imag + c_imag * q_real
                else:
                    new_real = c_real * q_real + c_imag * q_imag
                    new_imag = c_real * q_imag - c_imag * q_real
                real = new_real if term == 0 else real + new_real
                imag = new_imag if term == 0 else imag + new_imag
            target[kind, 0, freq, cells, :] = real
            target[kind, 1, freq, cells, :] = imag
            field_real = fields[tick, 0, 0, freq, cells, :]
            field_imag = fields[tick, 0, 1, freq, cells, :]
            if kind == 0:
                illum[cells, :] += field_real * field_real + field_imag * field_imag
            else:
                corr[cells, :] += (
                    field_real * fields[tick, 1, 0, freq, cells, :]
                    + field_imag * fields[tick, 1, 1, freq, cells, :]
                )

    def inject_source(tick):
        if tick == 0:
            small[2].wait()
            small[3].wait()
        grid_x = lax.broadcasted_iota(jnp.int32, (width, width), 0)
        grid_y = lax.broadcasted_iota(jnp.int32, (width, width), 1)
        hits = [
            (grid_x == src_pos[tick, 0, e]) & (grid_y == src_pos[tick, 1, e])
            for e in range(src_pos.shape[2])
        ]
        for part in range(2):
            for freq in range(freqs):
                plane = jnp.zeros((width, width), jnp.float32)
                for e, hit in enumerate(hits):
                    plane = plane + jnp.where(hit, wavelet[tick, e, part, freq], 0.0)
                fields[tick + 1, 0, part, freq] = plane

    def inject_receiver(tick):
        if tick == 0:
            small[4].wait()
            small[5].wait()
        receivers = rec_pos.shape[1]
        cell = lax.broadcasted_iota(jnp.int32, (width, receivers), 0)
        hits_x = jnp.where(cell == rec_pos[0:1, :], 1.0, 0.0).astype(jnp.bfloat16)
        hits_y = jnp.where(cell == rec_pos[1:2, :], 1.0, 0.0).astype(jnp.bfloat16)
        for part in range(2):
            stacked = []
            for freq in range(freqs):
                weights = rec_data[tick, part, freq : freq + 1, :]
                for _ in range(3):
                    piece = weights.astype(jnp.bfloat16)
                    weights = weights - piece.astype(jnp.float32)
                    stacked.append(hits_x * piece)
            product = lax.dot_general(
                jnp.concatenate(stacked, axis=0),
                hits_y,
                (((1,), (1,)), ((), ())),
                preferred_element_type=jnp.float32,
            )
            for freq in range(freqs):
                low = 3 * freq * width
                fields[tick + 1, 1, part, freq] = (
                    product[low : low + width]
                    + product[low + width : low + 2 * width]
                    + product[low + 2 * width : low + 3 * width]
                )

    small[1].wait()
    for kind in range(2):
        for tick in range(ticks):
            if tick > 0:
                inject = inject_source if kind == 0 else inject_receiver
                pl.when(is_first)(functools.partial(inject, tick - 1))

            def chunk(freq, carry, tick=tick, kind=kind):
                if kind == 0:
                    gather_coefficients(tick, freq)
                if tick == 0:
                    load_copy(kind, freq).wait()
                else:

                    @pl.when(position > 0)
                    def _():
                        send_copy(tick - 1, kind, freq).wait_recv()

                depth_step(tick, kind, freq)
                if tick == 0 and kind == 0:

                    @pl.when(freq == 0)
                    def _():
                        pl.semaphore_wait(barrier, greetings)

                if tick < ticks - 1:

                    @pl.when(has_next)
                    def _():
                        send_copy(tick, kind, freq).start()
                else:
                    out_copy(kind, freq).start()
                for stage in range(1, stages + 1):
                    turn = 2 * stage - 1
                    if stage < stages and kind == 1 and tick == turn // freqs:
                        pl.when(freq == turn % freqs)(functools.partial(exchange, stage))
                return carry

            lax.fori_loop(0, freqs, chunk, 0)
            if kind == 0 and tick == ticks - 1:
                running[0] = jnp.sum(illum[...].reshape(width // 8, 8, width), axis=0)
                exchange(0)

    exchange(stages)
    energy = jnp.sum(running[stages], keepdims=True)
    damping = energy / (chain * width * width)
    image[0] = math.sqrt(ticks * freqs) * corr[...] / (illum[...] + damping)

    for stage in range(stages):
        total_copy(stage).wait_send()

    @pl.when(jnp.logical_not(is_first))
    def _():
        for copy in small[2:]:
            copy.wait()

    for kind in range(2):
        for freq in range(freqs):
            for tick in range(ticks - 1):

                @pl.when(has_next)
                def _():
                    send_copy(tick, kind, freq).wait_send()

            out_copy(kind, freq).wait()


def solution(mesh):
    chain = mesh.shape["depth"]

    def body(arriving, classes, filters, src_pos, wavelet, rec_pos, rec_data):
        _, kinds, parts, freqs, width, _ = arriving.shape
        ticks = wavelet.shape[0] + 1
        terms, labels = filters.shape[3:]
        blocks = filters.shape[0]
        columns = filters.transpose(1, 2, 3, 4, 0).reshape(-1, blocks)
        f32 = jnp.float32
        stages = chain.bit_length() - 1
        vmem = pl.BlockSpec(memory_space=pltpu.VMEM)
        hbm = pl.BlockSpec(memory_space=pltpu.HBM)
        window = (ticks, kinds, parts, freqs, width, width)
        return pl.pallas_call(
            functools.partial(kernel, chain, ticks, freqs, terms, labels, width),
            out_shape=(
                jax.ShapeDtypeStruct((1, width, width), f32),
                jax.ShapeDtypeStruct(arriving.shape, f32),
            ),
            in_specs=[hbm] * 7,
            out_specs=(vmem, hbm),
            scratch_shapes=[
                pltpu.SMEM(src_pos.transpose(0, 2, 1).shape, jnp.int32),
                pltpu.SMEM(wavelet.shape, f32),
                pltpu.VMEM(classes.shape, jnp.int32),
                pltpu.VMEM(columns.shape, f32),
                pltpu.VMEM(rec_pos.T.shape, jnp.int32),
                pltpu.VMEM(rec_data.shape, f32),
                pltpu.VMEM(window, f32),
                pltpu.VMEM(window, f32),
                pltpu.VMEM((freqs * parts * terms, pl.cdiv(blocks, 8) * 8, width), f32),
                pltpu.VMEM((ticks, freqs, parts, terms, width, width), f32),
                pltpu.VMEM((parts, terms, width + 2 * PAD, width), f32),
                pltpu.VMEM((width, width), f32),
                pltpu.VMEM((width, width), f32),
                pltpu.VMEM((stages + 1, 8, width), f32),
                pltpu.VMEM((stages, 8, width), f32),
                pltpu.SemaphoreType.DMA((kinds, freqs)),
                pltpu.SemaphoreType.DMA((6,)),
                pltpu.SemaphoreType.DMA((kinds, freqs)),
                pltpu.SemaphoreType.DMA((ticks - 1, kinds, freqs)),
                pltpu.SemaphoreType.DMA((ticks - 1, kinds, freqs)),
                pltpu.SemaphoreType.DMA((stages,)),
                pltpu.SemaphoreType.DMA((stages,)),
            ],
            compiler_params=pltpu.CompilerParams(
                collective_id=0, has_side_effects=True, vmem_limit_bytes=67043328 - 1200000
            ),
        )(src_pos.transpose(0, 2, 1), wavelet, arriving, classes, columns, rec_pos.T, rec_data)

    return jax.shard_map(
        body,
        mesh=mesh,
        in_specs=(
            P(("survey", "depth"), None, None, None, None, None),
            P("depth", None, None),
            P(),
            P("survey", None, None),
            P("survey", None, None, None),
            P("survey", None),
            P("survey", None, None, None),
        ),
        out_specs=(
            P(("survey", "depth"), None, None),
            P(("survey", "depth"), None, None, None, None, None),
        ),
        check_vma=False,
    )
```

time: 41 us -> 36.3 us (0.89)
  Pallas kernels: 35.8 us -> 31.7 us
  local copies, waits for them, and re-layouts: 4.32 us -> 3.77 us
    pallas_call x1, Pallas kernels: 35.8 us -> 31.7 us  [body(): pl.pallas_call(functools.partial(kernel, chain, ticks, freqs, terms, labe...]
    unnamed x15 -> x2, local copies, waits for them, and re-layouts: 4.32 us -> 3.77 us
where the time goes in v1:
time: 36.3 us; the launch traced here: 36.1 us
  Pallas kernels  31.7 us (87%)
  local copies, waits for them, and re-layouts  3.77 us (10%)
  between operations  0.64 us (2%)
    pallas_call x1, Pallas kernels, body(): pl.pallas_call(functools.partial(kernel, chain, ticks, freqs, terms, labe...  31.7 us
    unnamed x2, local copies, waits for them, and re-layouts  3.77 us

profile of v1, /device:TPU:0, one launch (start us, length us, event | category | flops | bytes accessed | tf_op | source)
XLA Modules:
  0.0 36.1 jit_solution(17655785112407704603)
XLA Ops:
  0.6 31.7 %shard_map.86 = (f32[1,128,128]{2,1,0:T(8,128)}, f32[1,2,2,4,128,128]{5,4,3,2,1,0:T(8,128)}) custom-call(s32[2,2,4]{2,1,0:T(2,128)} %bitcast.7, f32[2,4,2,4]{3,2,1,0:T(2,128)} %wavelet_in.1, f32[1,2,2,4,128,128]{5,4,3,2,1,0:T(8,128)} %arriving.1, s32[1,128,128]{2,1,0:T(8,128)} %classes_in.1, f32[768,18]{1,0:T(8,128)} %bitcast.5, s32[2,512]{1,0:T(2,128)} %bitcast.6, ...), custom_call_target="tpu_custom_call" | custom-call | tf_op jit(solution)/shard_map/pallas_call | solution.py:361
  32.3 1.5 %copy.11 = f32[1,128,128]{2,1,0:T(8,128)} copy(f32[1,128,128]{2,1,0:T(8,128)} %get-tuple-element.4) | data formatting | bytes 131072
  33.8 2.3 %copy.12 = f32[1,2,2,4,128,128]{5,4,3,2,1,0:T(8,128)} copy(f32[1,2,2,4,128,128]{5,4,3,2,1,0:T(8,128)} %get-tuple-element.5) | data formatting | bytes 2097152

commit v2 on v1

--- a/solution.py
+++ b/solution.py
@@ -391,9 +391,22 @@
                 pltpu.SemaphoreType.DMA((stages,)),
             ],
             compiler_params=pltpu.CompilerParams(
-                collective_id=0, has_side_effects=True, vmem_limit_bytes=67043328 - 1200000
+                collective_id=0, has_side_effects=True, vmem_limit_bytes=67043328 - 20000000
             ),
-        )(src_pos.transpose(0, 2, 1), wavelet, arriving, classes, columns, rec_pos.T, rec_data)
+        )(
+            *(
+                pltpu.with_memory_space_constraint(operand, pltpu.HBM)
+                for operand in (
+                    src_pos.transpose(0, 2, 1),
+                    wavelet,
+                    arriving,
+                    classes,
+                    columns,
+                    rec_pos.T,
+                    rec_data,
+                )
+            )
+        )
 
     return jax.shard_map(
         body,

time: 36.3 us -> 33.4 us (0.920)
  local copies, waits for them, and re-layouts: 3.77 us -> 1.6 us
  Pallas kernels: 31.7 us -> 31 us
    unnamed x2, local copies, waits for them, and re-layouts: 3.77 us -> 1.6 us
    pallas_call x1, Pallas kernels: 31.7 us -> 31 us  [body(): pl.pallas_call(functools.partial(kernel, chain, ticks, freqs, terms, labe...]
where the time goes in v2:
time: 33.4 us; the launch traced here: 33.2 us
  Pallas kernels  31 us (93%)
  local copies, waits for them, and re-layouts  1.6 us (5%)
  between operations  0.64 us (2%)
    pallas_call x1, Pallas kernels, body(): pl.pallas_call(functools.partial(kernel, chain, ticks, freqs, terms, labe...  31 us
    unnamed x2, local copies, waits for them, and re-layouts  1.6 us

profile of v2, /device:TPU:0, one launch (start us, length us, event | category | flops | bytes accessed | tf_op | source)
XLA Modules:
  0.0 33.2 jit_solution(12847225611628305745)
XLA Ops:
  0.6 31.0 %shard_map.86 = (f32[1,128,128]{2,1,0:T(8,128)S(1)}, f32[1,2,2,4,128,128]{5,4,3,2,1,0:T(8,128)S(1)}) custom-call(s32[2,2,4]{2,1,0:T(2,128)} %bitcast.7, f32[2,4,2,4]{3,2,1,0:T(2,128)} %wavelet_in.1, f32[1,2,2,4,128,128]{5,4,3,2,1,0:T(8,128)} %arriving.1, s32[1,128,128]{2,1,0:T(8,128)} %classes_in.1, f32[768,18]{1,0:T(8,128)} %bitcast.5, s32[2,512]{1,0:T(2,128)} %bitcast.6, ...), custom_call_target="tpu_custom_call" | custom-call | tf_op jit(solution)/shard_map/pallas_call | solution.py:361
  31.6 0.6 %copy.11 = f32[1,128,128]{2,1,0:T(8,128)} copy(f32[1,128,128]{2,1,0:T(8,128)S(1)} %get-tuple-element.4) | data formatting | bytes 131072
  32.3 1.0 %copy.12 = f32[1,2,2,4,128,128]{5,4,3,2,1,0:T(8,128)} copy(f32[1,2,2,4,128,128]{5,4,3,2,1,0:T(8,128)S(1)} %get-tuple-element.5) | data formatting | bytes 2097152
